TPU v7x, 256 devices: a whole 4x4x8 slice. The times are simulated.
256 devices in a mesh: row: 8 (over z_lo, y), col: 32 (over x, z_hi, core).
Axes of the slice: x: 4, y: 4, z: 8 (z_hi: 4, z_lo: 2; z = z_hi * 2 + z_lo), core: 2. Of those that a mesh axis runs over, the one named last changes fastest.
Arguments:
- ancestor_inv: float32 [16384, 16384], P('row', 'col'), may hold values from -0.09375 to 0.09375
- factor_rows: float32 [16384, 768], P(('row', 'col')), may hold values from -1.2 to 1.2
- diagonal_inv: float32 [3, 256, 256], replicated, may hold values from -6 to 6
- fill_list: int32 [3, 64], replicated, may hold values 0 or 1
Outputs:
- column_block: float32 [16384, 768], P(('row', 'col'))
- diagonal_block: float32 [3, 256, 256], replicated
All inputs are finite; a program needn't handle non-finite values.
Results may differ from a plain program's by a relative error of at most 0.000071.
Values sent between devices are 32-bit elements; how exact they have to be, the bound alone decides.
A program may use at most 64 MiB of HBM per device.

v0:
```python
import jax
import jax.numpy as jnp
from jax import lax
from jax.sharding import PartitionSpec as P

W = 256
SIBS = 3
TILE = 256


def spread(block, axis, holder):
    block = jnp.where(lax.axis_index(axis) == holder, block, jnp.zeros_like(block))
    return lax.psum(block, axis)


def row_masks(fill_list, first_row, row_count):
    positions = first_row + jnp.arange(row_count, dtype=jnp.int32)
    tile_index = positions // TILE
    one_hot = (
        tile_index[:, None] == jnp.arange(fill_list.shape[1], dtype=jnp.int32)[None, :]
    ).astype(jnp.float32)
    return jnp.dot(one_hot, fill_list.T.astype(jnp.float32), precision=lax.Precision.HIGHEST)


def local(ancestor_inv, factor_rows, diagonal_inv, fill_list):
    row_devices = lax.axis_size("row")
    col_devices = lax.axis_size("col")
    group_span = col_devices // row_devices
    own_rows = factor_rows.shape[0]
    band_rows = ancestor_inv.shape[0]
    block_rows = ancestor_inv.shape[1]
    row_index = lax.axis_index("row")
    col_index = lax.axis_index("col")
    first_row = row_index * band_rows + col_index * own_rows
    local_mask = row_masks(fill_list, first_row, own_rows)
    wide_mask = jnp.repeat(local_mask, W, axis=1)
    masked = factor_rows * wide_mask
    band = lax.all_gather(masked, "col", axis=0, tiled=True)
    offset = col_index % group_span * block_rows
    section = lax.dynamic_slice_in_dim(band, offset, block_rows, 0)
    factor_block = spread(section, "row", col_index // group_span)
    summed = lax.psum_scatter(
        jnp.dot(ancestor_inv, factor_block, precision=lax.Precision.HIGHEST),
        "col",
        scatter_dimension=0,
        tiled=True,
    )
    column_block = -summed * wide_mask
    left_side = masked.reshape(own_rows, SIBS, W)
    right_side = column_block.reshape(own_rows, SIBS, W)
    local_term = jnp.einsum("rkw,rkv->kwv", left_side, right_side, precision=lax.Precision.HIGHEST)
    update = lax.psum(local_term, ("row", "col"))
    return (column_block, diagonal_inv - update)


def solution(mesh):
    placed = (P("row", "col"), P(("row", "col"), None), P(), P())
    return jax.shard_map(
        local, mesh=mesh, in_specs=placed, out_specs=(P(("row", "col"), None), P()), check_vma=False
    )
```

profile of v0, /device:TPU:1, one launch (start us, length us, event | category | flops | bytes accessed | tf_op | source)
XLA Modules:
  0.0 577.2 jit_solution(12936478042979415377)
XLA Ops:
  7.2 0.0 all-gather.2.cloned.1.call-start
  7.2 0.9 fusion.5
  8.1 0.1 broadcast_in_dim.8
  8.3 1.6 mul.17
  9.9 0.0 all-gather.2.cloned.1.call-update
  10.0 0.0 all-reduce.3.cloned.1.call-start
  10.0 74.2 %all-gather.2.cloned.1.call-done = f32[2048,768]{1,0:T(8,128)} async-done(((f32[64,768]{1,0:T(8,128)}), f32[2048,768]{1,0:T(8,128)}) %all-gather.2.cloned.1.call-update) | async-done | bytes 6291472 | tf_op jit(solution)/shard_map/all_gather | solution.py:38
  84.3 2.7 dynamic-slice_select_fusion
  87.0 0.0 all-reduce.3.cloned.1.call-update
  87.1 0.0 reduce-scatter.4.cloned.1.call-start
  87.1 78.3 %all-reduce.3.cloned.1.call-done = f32[512,768]{1,0:T(8,128)} async-done(((f32[512,768]{1,0:T(8,128)}), f32[512,768]{1,0:T(8,128)}) %all-reduce.3.cloned.1.call-update) | async-done | bytes 1572880 | tf_op jit(solution)/shard_map/psum | solution.py:13
  165.4 23.7 %convolution_bitcast_fusion = f32[2048,768]{0,1:T(8,128)} fusion(f32[512,768]{1,0:T(8,128)} %all-reduce.3.cloned.1.call-done, f32[2048,512]{1,0:T(8,128)} %param.4), kind=kOutput, calls=%fused_computation | convolution fusion | flops 9663676416 | bytes 12058624 | tf_op jit(solution)/shard_map/dot_general | solution.py:43
  189.1 6.6 %copy.19 = f32[2048,768]{1,0:T(8,128)} copy(f32[2048,768]{0,1:T(8,128)} %convolution_bitcast_fusion) | data formatting | bytes 12582912
  195.7 0.0 copy-start
  195.7 0.0 copy-start.2
  195.7 0.0 reduce-scatter.4.cloned.1.call-update
  195.7 0.0 all-reduce.5.cloned.1.call-start
  195.7 112.1 %reduce-scatter.4.cloned.1.call-done = f32[64,768]{1,0:T(8,128)} async-done(((f32[2048,768]{1,0:T(8,128)}), f32[64,768]{1,0:T(8,128)}) %reduce-scatter.4.cloned.1.call-update) | async-done | bytes 196624 | tf_op jit(solution)/shard_map/reduce_scatter | solution.py:42
  307.8 0.9 negate_multiply_fusion
  308.8 0.0 copy-start.1
  308.8 0.0 copy-done
  308.8 1.7 fusion
  310.5 0.0 all-reduce.5.cloned.1.call-update
  310.6 258.0 %all-reduce.5.cloned.1.call-done = f32[3,256,256]{2,1,0:T(8,128)} async-done(((f32[3,256,256]{2,1,0:T(8,128)}), f32[3,256,256]{2,1,0:T(8,128)}) %all-reduce.5.cloned.1.call-update) | async-done | bytes 786448 | tf_op jit(solution)/shard_map/psum | solution.py:52
  568.5 0.0 copy-done.2
  568.5 2.1 sub.15
  570.6 0.0 copy-done.1
  (2 shorter events, 0.0 us)
Async XLA Ops:
  7.2 77.1 %all-gather.2.cloned.1.call-start = ((), (), s32[]{:S(2)}) async-start(), calls=%async_computation.1 | async-start | bytes 6488064 | tf_op jit(solution)/shard_map/all_gather | solution.py:38
  10.0 155.5 %all-reduce.3.cloned.1.call-start = ((), (), s32[]{:S(2)}) async-start(), calls=%async_computation.2 | async-start | bytes 3145728 | tf_op jit(solution)/shard_map/psum | solution.py:13
  87.1 220.8 %reduce-scatter.4.cloned.1.call-start = ((), (), s32[]{:S(2)}) async-start(), calls=%async_computation.4 | async-start | bytes 6488064 | tf_op jit(solution)/shard_map/reduce_scatter | solution.py:42
  195.7 113.2 %copy-start = (f32[64,768]{1,0:T(8,128)S(1)}, f32[64,768]{1,0:T(8,128)}, u32[]{:S(2)}) copy-start(f32[64,768]{1,0:T(8,128)} %mul.17) | copy-start | bytes 589828
  195.7 372.9 %copy-start.2 = (f32[3,256,256]{2,1,0:T(8,128)S(1)}, f32[3,256,256]{2,1,0:T(8,128)}, u32[]{:S(2)}) copy-start(f32[3,256,256]{2,1,0:T(8,128)} %param.6) | copy-start | bytes 2359300
  195.7 372.8 %all-reduce.5.cloned.1.call-start = ((), (), s32[]{:S(2)}) async-start(), calls=%async_computation.3 | async-start | bytes 1572864 | tf_op jit(solution)/shard_map/psum | solution.py:52
  308.8 261.8 %copy-start.1 = (f32[64,768]{1,0:T(8,128)}, f32[64,768]{1,0:T(8,128)S(1)}, u32[]{:S(2)}) copy-start(f32[64,768]{1,0:T(8,128)S(1)} %negate_multiply_fusion) | copy-start | bytes 589828
Sparse Core Ops, SparseCore 0:
  11.1 73.1 all-gather.1
  87.2 78.2 all-reduce.2
  195.8 111.9 reduce-scatter.3
  313.7 254.7 all-reduce.4
where the time goes:
time: 578 us; the launch traced here: 577 us
  waiting for transfers between devices  523 us (90%)
  matrix products  26.3 us (5%)
  between operations  13.9 us (2%)
  other arithmetic  7.44 us (1%)
  local copies, waits for them, and re-layouts  6.73 us (1%)
    psum x1, waiting for transfers between devices, local(): update = lax.psum(local_term, ('row', 'col'))  258 us
    reduce_scatter x1, waiting for transfers between devices, local(): lax.psum_scatter(jnp.dot(ancestor_inv, factor_block, precision=lax.Precis...  112 us
    psum x1, waiting for transfers between devices, spread(): return lax.psum(block, axis)  78.3 us
    all_gather x1, waiting for transfers between devices, local(): band = lax.all_gather(masked, 'col', axis=0, tiled=True)  74.2 us
    dot_general x1, matrix products, local(): jnp.dot(ancestor_inv, factor_block, precision=lax.Precision.HIGHEST)  23.7 us
  transfers between devices with their start and end apart: 4, of which 4 were waited for; matrix products, arithmetic and copies ran while one was open for 0% of the time, Pallas kernels for 0%

commit v1 on v0

v1 whole, which is shorter than its diff:
```python
import functools

import jax
import jax.numpy as jnp
from jax import lax
from jax.experimental import pallas as pl
from jax.experimental.pallas import tpu as pltpu
from jax.sharding import PartitionSpec as P

W = 256
SIBS = 3
HALF = 128
F32 = jnp.float32
BF16 = jnp.bfloat16


def split(v):
    high = v.astype(BF16)
    return high, (v - high.astype(F32)).astype(BF16)


def three_pass(a_high, a_low, b_high, b_low):
    dot = functools.partial(jnp.dot, preferred_element_type=F32)
    return dot(a_high, b_high) + (dot(a_high, b_low) + dot(a_low, b_high))


def kernel(
    fill, fac, a_in, d_in, cb, dg,
    a_own, a_rec, a_high, a_low, m_own, m_rec, m_high, m_low, f_own, f_rec, t_high, t_low, d_slab,
    prod, xa, xr, zb, c_own, c_rec, u, rs, zs, g,
    local_sem, perm_s, perm_r, one_s, one_r, ag_s, ag_r, x_s, x_r, z_s, z_r, c_s, c_r,
    p_s, p_r, e_s, e_r, q_s, q_r, h_s, h_r,
):
    r = lax.axis_index("row")
    c = lax.axis_index("col")
    zl, y = lax.div(r, 4), lax.rem(r, 4)
    x, zh, core = lax.div(c, 8), lax.rem(lax.div(c, 2), 4), lax.rem(c, 2)
    z = zh * 2 + zl
    other = 1 - core
    slab = x * 4 + y

    def wrap(v, n):
        return lax.rem(v + n, n)

    def at(x_, y_, z_, core_):
        return (lax.rem(z_, 2) * 4 + y_, x_ * 8 + lax.div(z_, 2) * 2 + core_)

    def swap(v):
        return v + 1 - 2 * lax.rem(v, 2)

    partner = at(x, y, z, other)
    y_up, y_down = wrap(y + 1, 4), wrap(y - 1, 4)
    y_far = wrap(y + 2, 4)
    up, down = at(x, y_up, z, core), at(x, y_down, z, core)
    right, left = at(wrap(x + 1, 4), y, z, core), at(wrap(x - 1, 4), y, z, core)
    twin = at(x, y, zh * 2 + 1 - zl, core)
    piece = lax.rem(c, 8)
    target = (swap(piece), r * 4 + x)
    source_index = c * 8 + swap(r)
    source = (lax.div(source_index, 32), lax.rem(source_index, 32))

    def plane(d):
        return wrap(x + lax.div(d, 4), 4), wrap(y + lax.rem(d, 4), 4)

    barrier = pltpu.get_barrier_semaphore()

    def hello(device):
        pl.semaphore_signal(barrier, inc=1, device_id=device, device_id_type=pl.DeviceIdType.MESH)

    @pl.loop(1, 16)
    def _(d):
        px, py = plane(d)
        hello(at(px, py, z, core))

    @pl.loop(1, 8)
    def _(d):
        hello(at(x, y, wrap(z + d, 8), core))

    hello(partner)
    hello(target)
    hello(source)

    own_rows = pltpu.make_async_copy(a_in.at[:, core], a_own, local_sem.at[0])
    own_rows.start()
    own_factor = pltpu.make_async_copy(fac, f_own, local_sem.at[1])
    own_factor.start()
    own_diag = pltpu.make_async_copy(
        d_in.at[:, pl.ds(pl.multiple_of(slab * 16, 16), 16), pl.ds(pl.multiple_of(core * HALF, HALF), HALF)],
        d_slab,
        local_sem.at[2],
    )
    own_diag.start()
    pl.semaphore_wait(barrier, 25)

    sent = []

    def copy(src, dst, ssem, rsem, device):
        return pltpu.make_async_remote_copy(
            src_ref=src, dst_ref=dst, send_sem=ssem, recv_sem=rsem,
            device_id=device, device_id_type=pl.DeviceIdType.MESH,
        )

    def send(src, dst, ssem, rsem, device):
        out = copy(src, dst, ssem, rsem, device)
        out.start()
        sent.append(out)

    def arrived(dst, ssem, rsem):
        copy(dst, dst, ssem, rsem, partner).wait_recv()

    yme, ydn, yup, yfar = swap(y), swap(y_down), swap(y_up), swap(y_far)
    for k in range(SIBS):
        landing = m_own.at[k, lax.rem(piece, 4), lax.div(piece, 4)]
        send(fac.at[:, pl.ds(k * W, W)], landing, perm_s.at[k], perm_r.at[k], target)
    send(a_in.at[:, other], a_rec, one_s.at[0], one_r.at[0], partner)
    send(fac, f_rec, one_s.at[1], one_r.at[1], partner)

    def split_rows(src, column):
        @pl.loop(0, 16)
        def _(i):
            rows = pl.ds(pl.multiple_of(i * 64, 64), 64)
            high, low = split(src[i])
            a_high[rows, column : column + 512] = high
            a_low[rows, column : column + 512] = low

    def ag(k, n, src, dst, device):
        send(src, dst, ag_s.at[k, n], ag_r.at[k, n], device)

    def ag_in(k, n, dst):
        arrived(dst, ag_s.at[k, n], ag_r.at[k, n])

    def gather_a(k):
        own = m_own.at[k, yme, zl]
        arrived(own, perm_s.at[k], perm_r.at[k])
        ag(k, 0, own, own, twin)
        ag(k, 1, own, own, up)
        ag(k, 2, own, own, down)
        ag(k, 3, own, m_rec.at[k, yme, zl], partner)

    def gather_b(k):
        own = m_own.at[k, yme, 1 - zl]
        ag_in(k, 0, own)
        ag(k, 4, own, own, up)
        ag(k, 5, own, own, down)
        ag(k, 6, own, m_rec.at[k, yme, 1 - zl], partner)

    def gather_c(k):
        low = m_own.at[k, ydn, zl]
        ag_in(k, 1, low)
        ag(k, 7, low, low, up)
        high = m_own.at[k, yup, 1 - zl]
        ag_in(k, 5, high)
        ag(k, 8, high, high, down)

    def gather_d(k):
        ag_in(k, 4, m_own.at[k, ydn, 1 - zl])
        ag(k, 9, m_own.at[k, ydn], m_rec.at[k, ydn], partner)
        ag_in(k, 2, m_own.at[k, yup, zl])
        ag(k, 10, m_own.at[k, yup], m_rec.at[k, yup], partner)
        ag_in(k, 7, m_own.at[k, yfar, zl])
        ag_in(k, 8, m_own.at[k, yfar, 1 - zl])
        ag(k, 11, m_own.at[k, yfar], m_rec.at[k, yfar], partner)

    def split_pieces(k, src, column, first):
        for half in range(2):
            mask = fill[k, 2 * column + half].astype(F32)
            for n in range(4):
                row = first + (half * 4 + n) * 64
                high, low = split(src[k, n, half] * mask)
                m_high[k, row : row + 64] = high
                m_low[k, row : row + 64] = low

    def gather_e(k):
        split_pieces(k, m_own, c, 0)
        ag_in(k, 3, m_rec.at[k, yme, zl])
        ag_in(k, 6, m_rec.at[k, yme, 1 - zl])
        ag_in(k, 9, m_rec.at[k, ydn])
        ag_in(k, 10, m_rec.at[k, yup])
        ag_in(k, 11, m_rec.at[k, yfar])
        split_pieces(k, m_rec, swap(c), 512)

    own_tile = r * 8 + lax.div(c, 4)

    def own_masks():
        own_factor.wait()
        arrived(f_rec, one_s.at[1], one_r.at[1])
        for k in range(SIBS):
            mask = fill[k, own_tile].astype(F32)
            for n, src in enumerate((f_own, f_rec)):
                turned = (src[:, k * W : (k + 1) * W] * mask).T
                high, low = split(turned)
                t_high[k, :, n * 64 : (n + 1) * 64] = high
                t_low[k, :, n * 64 : (n + 1) * 64] = low

    def multiply(k, away):
        rows = pl.ds(pl.multiple_of(wrap(x + away, 4) * 256, 256), 256)
        result = three_pass(a_high[rows, :], a_low[rows, :], m_high[k], m_low[k])
        prod[k, away] = result.reshape(4, 64, W)

    def xs(k, n, src, device):
        send(src, xa.at[k, n], x_s.at[k, n], x_r.at[k, n], device)

    def x_in(k, n):
        arrived(xa.at[k, n], x_s.at[k, n], x_r.at[k, n])

    def x_one(k):
        multiply(k, 2)
        xs(k, 0, prod.at[k, 2, pl.ds(0, 2)], right)
        xs(k, 1, prod.at[k, 2, pl.ds(2, 2)], left)

    def x_two(k):
        multiply(k, 1)
        xs(k, 2, prod.at[k, 1, pl.ds(2, 2)], right)
        multiply(k, 3)
        xs(k, 3, prod.at[k, 3, pl.ds(0, 2)], left)

    def x_three(k):
        x_in(k, 0)
        prod[k, 1, 0:2] = prod[k, 1, 0:2] + xa[k, 0]
        xs(k, 4, prod.at[k, 1, pl.ds(0, 2)], right)
        x_in(k, 1)
        prod[k, 3, 2:4] = prod[k, 3, 2:4] + xa[k, 1]
        xs(k, 5, prod.at[k, 3, pl.ds(2, 2)], left)

    def x_sum(k):
        x_in(k, 3)
        x_in(k, 4)
        xr[k, 0:2] = prod[k, 0, 0:2] + xa[k, 4] + xa[k, 3]
        x_in(k, 2)
        x_in(k, 5)
        xr[k, 2:4] = prod[k, 0, 2:4] + xa[k, 2] + xa[k, 5]
        for d in (2, 1, 3):
            there = wrap(zh + d, 4)
            send(xr.at[k, there], zb.at[k, d - 1], z_s.at[k, d - 1], z_r.at[k, d - 1], at(x, y, there * 2 + zl, core))

    def z_sum(k):
        for d in range(3):
            arrived(zb.at[k, d], z_s.at[k, d], z_r.at[k, d])
        mask = fill[k, own_tile].astype(F32)
        block = -(xr[k, zh] + zb[k, 0] + zb[k, 1] + zb[k, 2]) * mask
        cb[:, k * W : (k + 1) * W] = block
        c_own[k, 0] = block[:, :HALF]
        c_own[k, 1] = block[:, HALF:]
        send(c_own.at[k, other], c_rec.at[k], c_s.at[k], c_r.at[k], partner)

    def local_term(k):
        t_h, t_l = t_high[k], t_low[k]
        arrived(c_rec.at[k], c_s.at[k], c_r.at[k])
        high, low = split(jnp.concatenate([c_own[k, core], c_rec[k]], axis=0))
        u[k] = three_pass(t_h, t_l, high, low).reshape(16, 16, HALF)

        @pl.loop(1, 16)
        def _(d):
            px, py = plane(d)
            copy(u.at[k, px * 4 + py], rs.at[k, d], p_s.at[k, d], p_r.at[k, d], at(px, py, z, core)).start()

    def plane_sum(k):
        total = u[k, slab]
        for d in range(1, 16):
            arrived(rs.at[k, d], p_s.at[k, d], p_r.at[k, d])
            total = total + rs[k, d]
        zs[k, z] = total

        @pl.loop(1, 8)
        def _(d):
            to = at(x, y, wrap(z + d, 8), core)
            copy(zs.at[k, z], zs.at[k, z], e_s.at[k, d], e_r.at[k, d], to).start()

    def line_sum(k):
        @pl.loop(1, 8)
        def _(d):
            arrived(zs.at[k, wrap(z - d, 8)], e_s.at[k, d], e_r.at[k, d])

        total = zs[k, 0]
        for n in range(1, 8):
            total = total + zs[k, n]
        g[k, core, slab] = d_slab[k] - total

        @pl.loop(1, 16)
        def _(d):
            px, py = plane(d)
            mine = g.at[k, core, slab]
            copy(mine, mine, q_s.at[k, d], q_r.at[k, d], at(px, py, z, core)).start()

    def spread(k):
        @pl.loop(1, 16)
        def _(d):
            px, py = wrap(x - lax.div(d, 4), 4), wrap(y - lax.rem(d, 4), 4)
            arrived(g.at[k, core, px * 4 + py], q_s.at[k, d], q_r.at[k, d])

        send(g.at[k, core], g.at[k, core], h_s.at[k], h_r.at[k], partner)

    def finish(k):
        arrived(g.at[k, other], h_s.at[k], h_r.at[k])
        dg[k, :, 0:HALF] = g[k, 0].reshape(W, HALF)
        dg[k, :, HALF:W] = g[k, 1].reshape(W, HALF)

    own_rows.wait()
    split_rows(a_own, 0)
    gather_a(0)
    gather_a(1)
    gather_b(0)
    gather_a(2)
    gather_c(0)
    gather_b(1)
    arrived(a_rec, one_s.at[0], one_r.at[0])
    split_rows(a_rec, 512)
    gather_d(0)
    gather_c(1)
    gather_b(2)
    gather_e(0)
    x_one(0)
    gather_d(1)
    x_two(0)
    gather_c(2)
    gather_e(1)
    x_one(1)
    gather_d(2)
    x_three(0)
    x_two(1)
    gather_e(2)
    x_one(2)
    own_diag.wait()
    own_masks()
    multiply(0, 0)
    x_three(1)
    x_two(2)
    multiply(1, 0)
    x_sum(0)
    multiply(2, 0)
    x_three(2)
    z_sum(0)
    local_term(0)
    x_sum(1)
    plane_sum(0)
    x_sum(2)
    z_sum(1)
    local_term(1)
    line_sum(0)
    z_sum(2)
    local_term(2)
    plane_sum(1)
    spread(0)
    line_sum(1)
    plane_sum(2)
    finish(0)
    spread(1)
    line_sum(2)
    finish(1)
    spread(2)
    finish(2)

    for out in sent:
        out.wait_send()
    for k in range(SIBS):

        @pl.loop(1, 16)
        def _(d):
            copy(u.at[k, 0], rs.at[k, d], p_s.at[k, d], p_r.at[k, d], partner).wait_send()
            copy(g.at[k, core, slab], g.at[k, core, slab], q_s.at[k, d], q_r.at[k, d], partner).wait_send()

        @pl.loop(1, 8)
        def _(d):
            copy(zs.at[k, z], zs.at[k, z], e_s.at[k, d], e_r.at[k, d], partner).wait_send()


def local(ancestor_inv, factor_rows, diagonal_inv, fill_list):
    vmem, dma = pltpu.VMEM, pltpu.SemaphoreType.DMA
    hbm = pl.BlockSpec(memory_space=pl.ANY)
    pairs = [(SIBS,), (2,), (SIBS, 12), (SIBS, 6), (SIBS, 3), (SIBS,), (SIBS, 16), (SIBS, 8), (SIBS, 16), (SIBS,)]
    return pl.pallas_call(
        kernel,
        out_shape=(
            jax.ShapeDtypeStruct(factor_rows.shape, F32),
            jax.ShapeDtypeStruct(diagonal_inv.shape, F32),
        ),
        in_specs=[pl.BlockSpec(memory_space=pltpu.SMEM), hbm, hbm, hbm],
        out_specs=[pl.BlockSpec(memory_space=pltpu.VMEM)] * 2,
        scratch_shapes=[
            vmem((16, 64, 512), F32),
            vmem((16, 64, 512), F32),
            vmem((1024, 1024), BF16),
            vmem((1024, 1024), BF16),
            vmem((SIBS, 4, 2, 64, W), F32),
            vmem((SIBS, 4, 2, 64, W), F32),
            vmem((SIBS, 1024, W), BF16),
            vmem((SIBS, 1024, W), BF16),
            vmem((64, SIBS * W), F32),
            vmem((64, SIBS * W), F32),
            vmem((SIBS, W, 128), BF16),
            vmem((SIBS, W, 128), BF16),
            vmem((SIBS, 16, HALF), F32),
            vmem((SIBS, 4, 4, 64, W), F32),
            vmem((SIBS, 6, 2, 64, W), F32),
            vmem((SIBS, 4, 64, W), F32),
            vmem((SIBS, 3, 64, W), F32),
            vmem((SIBS, 2, 64, HALF), F32),
            vmem((SIBS, 64, HALF), F32),
            vmem((SIBS, 16, 16, HALF), F32),
            vmem((SIBS, 16, 16, HALF), F32),
            vmem((SIBS, 8, 16, HALF), F32),
            vmem((SIBS, 2, 16, 16, HALF), F32),
            dma((3,)),
        ]
        + [dma(shape) for shape in pairs for _ in range(2)],
        compiler_params=pltpu.CompilerParams(
            collective_id=0, has_side_effects=True, vmem_limit_bytes=56 * 1024 * 1024
        ),
    )(fill_list, factor_rows, ancestor_inv.reshape(16, 2, 64, 512), diagonal_inv)


def solution(mesh):
    placed = (P("row", "col"), P(("row", "col"), None), P(), P())
    return jax.shard_map(
        local, mesh=mesh, in_specs=placed, out_specs=(P(("row", "col"), None), P()), check_vma=False
    )
```

time: 578 us -> 113 us (0.20)
  waiting for transfers between devices: 523 us -> 0 us
  Pallas kernels: 0 us -> 109 us
  matrix products: 26.3 us -> 0 us
  between operations: 13.9 us -> 0.64 us
  other arithmetic: 7.44 us -> 0 us
    psum x2 -> x0, waiting for transfers between devices: 336 us -> none  [the longest x1 258 us: local(): update = lax.psum(local_term, ('row', 'col'))]
    reduce_scatter x1 -> x0, waiting for transfers between devices: 112 us -> none  [local(): lax.psum_scatter(jnp.dot(ancestor_inv, factor_block, precision=lax.Precis...]
    pallas_call x0 -> x1, Pallas kernels: none -> 109 us  [local(): pl.pallas_call(kernel, out_shape=(jax.ShapeDtypeStruct(factor_rows.shape,...]
    all_gather x1 -> x0, waiting for transfers between devices: 74.2 us -> none  [local(): band = lax.all_gather(masked, 'col', axis=0, tiled=True)]
    dot_general x3 -> x0, matrix products: 26.3 us -> none  [the longest x1 23.7 us: local(): jnp.dot(ancestor_inv, factor_block, precision=lax.Precision.HIGHEST)]
  transfers between devices with their start and end apart: 4 -> 0, of which waited for: 4 -> 0; matrix products, arithmetic and copies ran while one was open for 0% -> 0% of each run, Pallas kernels for 0% -> 0%
where the time goes in v1:
time: 113 us
  Pallas kernels  109 us (96%)
  local copies, waits for them, and re-layouts  3.68 us (3%)
    pallas_call x1, Pallas kernels, local(): pl.pallas_call(kernel, out_shape=(jax.ShapeDtypeStruct(factor_rows.shape,...  109 us
    unnamed x2, local copies, waits for them, and re-layouts  3.68 us

profile of v1, /device:TPU:1, one launch (start us, length us, event | category | flops | bytes accessed | tf_op | source)
XLA Modules:
  0.0 113.3 jit_solution(6877285919746649730)
XLA Ops:
  0.6 108.9 %shard_map.59 = (f32[64,768]{1,0:T(8,128)}, f32[3,256,256]{2,1,0:T(8,128)}) custom-call(s32[3,64]{1,0:T(4,128)} %fill.1, f32[64,768]{1,0:T(8,128)} %fac.1, f32[16,2,64,512]{3,2,1,0:T(8,128)} %bitcast.1, f32[3,256,256]{2,1,0:T(8,128)} %d_in.1), custom_call_target="tpu_custom_call" | custom-call | tf_op jit(solution)/shard_map/pallas_call | solution.py:371
  109.6 1.6 %copy.8 = f32[64,768]{1,0:T(8,128)} copy(f32[64,768]{1,0:T(8,128)} %get-tuple-element.4) | data formatting | bytes 393216
  111.2 2.1 %copy.9 = f32[3,256,256]{2,1,0:T(8,128)} copy(f32[3,256,256]{2,1,0:T(8,128)} %get-tuple-element.5) | data formatting | bytes 1572864

commit v2 on v1

--- a/solution.py
+++ b/solution.py
@@ -27,8 +27,8 @@
 def kernel(
     fill, fac, a_in, d_in, cb, dg,
     a_own, a_rec, a_high, a_low, m_own, m_rec, m_high, m_low, f_own, f_rec, t_high, t_low, d_slab,
-    prod, xa, xr, zb, c_own, c_rec, u, rs, zs, g,
-    local_sem, perm_s, perm_r, one_s, one_r, ag_s, ag_r, x_s, x_r, z_s, z_r, c_s, c_r,
+    turn, prod, xa, xr, zb, c_own, c_rec, u, rs, zs, g,
+    local_sem, turn_s, turn_r, perm_s, perm_r, one_s, one_r, ag_s, ag_r, x_s, x_r, z_s, z_r, c_s, c_r,
     p_s, p_r, e_s, e_r, q_s, q_r, h_s, h_r,
 ):
     r = lax.axis_index("row")
@@ -54,10 +54,15 @@
     up, down = at(x, y_up, z, core), at(x, y_down, z, core)
     right, left = at(wrap(x + 1, 4), y, z, core), at(wrap(x - 1, 4), y, z, core)
     twin = at(x, y, zh * 2 + 1 - zl, core)
-    piece = lax.rem(c, 8)
-    target = (swap(piece), r * 4 + x)
-    source_index = c * 8 + swap(r)
-    source = (lax.div(source_index, 32), lax.rem(source_index, 32))
+    part = lax.div(zh, 2) * 2 + core
+
+    def target(y_from):
+        z_to = (2 * lax.rem(y_from, 2) + lax.div(x, 2)) * 2 + 1 - lax.rem(zh, 2)
+        return at(2 * zl + lax.div(y_from, 2), y, z_to, lax.rem(x, 2))
+
+    def source(n):
+        z_from = ((n // 2) * 2 + 1 - zl) * 2 + lax.div(x, 2)
+        return at(2 * lax.rem(zh, 2) + core, y, z_from, n % 2)
 
     def plane(d):
         return wrap(x + lax.div(d, 4), 4), wrap(y + lax.rem(d, 4), 4)
@@ -77,8 +82,9 @@
         hello(at(x, y, wrap(z + d, 8), core))
 
     hello(partner)
-    hello(target)
-    hello(source)
+    for n in range(4):
+        hello(target(n))
+        hello(source(n))
 
     own_rows = pltpu.make_async_copy(a_in.at[:, core], a_own, local_sem.at[0])
     own_rows.start()
@@ -90,30 +96,6 @@
         local_sem.at[2],
     )
     own_diag.start()
-    pl.semaphore_wait(barrier, 25)
-
-    sent = []
-
-    def copy(src, dst, ssem, rsem, device):
-        return pltpu.make_async_remote_copy(
-            src_ref=src, dst_ref=dst, send_sem=ssem, recv_sem=rsem,
-            device_id=device, device_id_type=pl.DeviceIdType.MESH,
-        )
-
-    def send(src, dst, ssem, rsem, device):
-        out = copy(src, dst, ssem, rsem, device)
-        out.start()
-        sent.append(out)
-
-    def arrived(dst, ssem, rsem):
-        copy(dst, dst, ssem, rsem, partner).wait_recv()
-
-    yme, ydn, yup, yfar = swap(y), swap(y_down), swap(y_up), swap(y_far)
-    for k in range(SIBS):
-        landing = m_own.at[k, lax.rem(piece, 4), lax.div(piece, 4)]
-        send(fac.at[:, pl.ds(k * W, W)], landing, perm_s.at[k], perm_r.at[k], target)
-    send(a_in.at[:, other], a_rec, one_s.at[0], one_r.at[0], partner)
-    send(fac, f_rec, one_s.at[1], one_r.at[1], partner)
 
     def split_rows(src, column):
         @pl.loop(0, 16)
@@ -123,15 +105,63 @@
             a_high[rows, column : column + 512] = high
             a_low[rows, column : column + 512] = low
 
+    own_rows.wait()
+    split_rows(a_own, 0)
+    pl.semaphore_wait(barrier, 31)
+
+    sent = []
+
+    def copy(src, dst, ssem, rsem, device):
+        return pltpu.make_async_remote_copy(
+            src_ref=src, dst_ref=dst, send_sem=ssem, recv_sem=rsem,
+            device_id=device, device_id_type=pl.DeviceIdType.MESH,
+        )
+
+    def send(src, dst, ssem, rsem, device):
+        out = copy(src, dst, ssem, rsem, device)
+        out.start()
+        sent.append(out)
+
+    def arrived(dst, ssem, rsem):
+        copy(dst, dst, ssem, rsem, partner).wait_recv()
+
+    yme, ydn, yup, yfar = y, y_down, y_up, y_far
+
+    def quarter(k, n):
+        return fac.at[pl.ds(pl.multiple_of(n * 16, 16), 16), pl.ds(k * W, W)]
+
+    def forward(k, n, y_from, src):
+        landing = m_own.at[k, y, 1 - lax.rem(zh, 2), pl.ds(pl.multiple_of(part * 16, 16), 16)]
+        send(src, landing, perm_s.at[k, n], perm_r.at[k, part], target(y_from))
+
+    for k in range(SIBS):
+        for d in (2, 1, 3):
+            y_to = wrap(y + d, 4)
+            send(quarter(k, y_to), turn.at[k, y], turn_s.at[k, d - 1], turn_r.at[k, d - 1], at(x, y_to, z, core))
+        forward(k, 0, y, quarter(k, y))
+    send(a_in.at[:, other], a_rec, one_s.at[0], one_r.at[0], partner)
+    send(fac, f_rec, one_s.at[1], one_r.at[1], partner)
+
+    def split_received(_):
+        arrived(a_rec, one_s.at[0], one_r.at[0])
+        split_rows(a_rec, 512)
+
     def ag(k, n, src, dst, device):
         send(src, dst, ag_s.at[k, n], ag_r.at[k, n], device)
 
     def ag_in(k, n, dst):
         arrived(dst, ag_s.at[k, n], ag_r.at[k, n])
 
+    def turned(k):
+        for d in (1, 3, 2):
+            y_from = wrap(y - d, 4)
+            arrived(turn.at[k, y_from], turn_s.at[k, d - 1], turn_r.at[k, d - 1])
+            forward(k, d, y_from, turn.at[k, y_from])
+
     def gather_a(k):
         own = m_own.at[k, yme, zl]
-        arrived(own, perm_s.at[k], perm_r.at[k])
+        for n in range(4):
+            arrived(m_own.at[k, yme, zl, pl.ds(n * 16, 16)], perm_s.at[k, n], perm_r.at[k, n])
         ag(k, 0, own, own, twin)
         ag(k, 1, own, own, up)
         ag(k, 2, own, own, down)
@@ -162,13 +192,15 @@
         ag(k, 11, m_own.at[k, yfar], m_rec.at[k, yfar], partner)
 
     def split_pieces(k, src, column, first):
-        for half in range(2):
-            mask = fill[k, 2 * column + half].astype(F32)
-            for n in range(4):
-                row = first + (half * 4 + n) * 64
-                high, low = split(src[k, n, half] * mask)
-                m_high[k, row : row + 64] = high
-                m_low[k, row : row + 64] = low
+        for n in range(4):
+            mask = fill[k, 2 * column + n // 2].astype(F32)
+            for half in range(2):
+                piece = (n // 2) * 4 + (1 - half) * 2 + n % 2
+                for m in range(4):
+                    row = first + piece * 64 + m * 16
+                    high, low = split(src[k, m, half, n * 16 : n * 16 + 16] * mask)
+                    m_high[k, row : row + 16] = high
+                    m_low[k, row : row + 16] = low
 
     def gather_e(k):
         split_pieces(k, m_own, c, 0)
@@ -181,7 +213,8 @@
 
     own_tile = r * 8 + lax.div(c, 4)
 
-    def own_masks():
+    def own_masks(_):
+        own_diag.wait()
         own_factor.wait()
         arrived(f_rec, one_s.at[1], one_r.at[1])
         for k in range(SIBS):
@@ -196,6 +229,9 @@
         rows = pl.ds(pl.multiple_of(wrap(x + away, 4) * 256, 256), 256)
         result = three_pass(a_high[rows, :], a_low[rows, :], m_high[k], m_low[k])
         prod[k, away] = result.reshape(4, 64, W)
+
+    def x_own(k):
+        multiply(k, 0)
 
     def xs(k, n, src, device):
         send(src, xa.at[k, n], x_s.at[k, n], x_r.at[k, n], device)
@@ -295,60 +331,24 @@
         dg[k, :, 0:HALF] = g[k, 0].reshape(W, HALF)
         dg[k, :, HALF:W] = g[k, 1].reshape(W, HALF)
 
-    own_rows.wait()
-    split_rows(a_own, 0)
-    gather_a(0)
-    gather_a(1)
-    gather_b(0)
-    gather_a(2)
-    gather_c(0)
-    gather_b(1)
-    arrived(a_rec, one_s.at[0], one_r.at[0])
-    split_rows(a_rec, 512)
-    gather_d(0)
-    gather_c(1)
-    gather_b(2)
-    gather_e(0)
-    x_one(0)
-    gather_d(1)
-    x_two(0)
-    gather_c(2)
-    gather_e(1)
-    x_one(1)
-    gather_d(2)
-    x_three(0)
-    x_two(1)
-    gather_e(2)
-    x_one(2)
-    own_diag.wait()
-    own_masks()
-    multiply(0, 0)
-    x_three(1)
-    x_two(2)
-    multiply(1, 0)
-    x_sum(0)
-    multiply(2, 0)
-    x_three(2)
-    z_sum(0)
-    local_term(0)
-    x_sum(1)
-    plane_sum(0)
-    x_sum(2)
-    z_sum(1)
-    local_term(1)
-    line_sum(0)
-    z_sum(2)
-    local_term(2)
-    plane_sum(1)
-    spread(0)
-    line_sum(1)
-    plane_sum(2)
-    finish(0)
-    spread(1)
-    line_sum(2)
-    finish(1)
-    spread(2)
-    finish(2)
+    order = [
+        (turned, 0), (turned, 1), (gather_a, 0), (turned, 2),
+        (gather_b, 0), (gather_a, 1), (split_received, 0), (gather_c, 0),
+        (gather_b, 1), (gather_a, 2), (gather_d, 0), (gather_c, 1),
+        (gather_b, 2), (gather_e, 0), (x_one, 0), (x_two, 0),
+        (gather_d, 1), (gather_c, 2), (gather_e, 1), (x_one, 1),
+        (x_three, 0), (x_two, 1), (gather_d, 2), (gather_e, 2),
+        (x_one, 2), (x_three, 1), (x_two, 2), (x_own, 0),
+        (own_masks, 0), (x_own, 1), (x_sum, 0), (x_three, 2),
+        (x_own, 2), (z_sum, 0), (local_term, 0), (x_sum, 1),
+        (x_sum, 2), (z_sum, 1), (local_term, 1), (plane_sum, 0),
+        (z_sum, 2), (local_term, 2), (plane_sum, 1), (line_sum, 0),
+        (plane_sum, 2), (line_sum, 1), (spread, 0), (line_sum, 2),
+        (spread, 1), (spread, 2), (finish, 0), (finish, 1),
+        (finish, 2),
+    ]
+    for step, k in order:
+        step(k)
 
     for out in sent:
         out.wait_send()
@@ -367,7 +367,7 @@
 def local(ancestor_inv, factor_rows, diagonal_inv, fill_list):
     vmem, dma = pltpu.VMEM, pltpu.SemaphoreType.DMA
     hbm = pl.BlockSpec(memory_space=pl.ANY)
-    pairs = [(SIBS,), (2,), (SIBS, 12), (SIBS, 6), (SIBS, 3), (SIBS,), (SIBS, 16), (SIBS, 8), (SIBS, 16), (SIBS,)]
+    pairs = [(SIBS, 3), (SIBS, 4), (2,), (SIBS, 12), (SIBS, 6), (SIBS, 3), (SIBS,), (SIBS, 16), (SIBS, 8), (SIBS, 16), (SIBS,)]
     return pl.pallas_call(
         kernel,
         out_shape=(
@@ -390,6 +390,7 @@
             vmem((SIBS, W, 128), BF16),
             vmem((SIBS, W, 128), BF16),
             vmem((SIBS, 16, HALF), F32),
+            vmem((SIBS, 4, 16, W), F32),
             vmem((SIBS, 4, 4, 64, W), F32),
             vmem((SIBS, 6, 2, 64, W), F32),
             vmem((SIBS, 4, 64, W), F32),
@@ -404,7 +405,7 @@
         ]
         + [dma(shape) for shape in pairs for _ in range(2)],
         compiler_params=pltpu.CompilerParams(
-            collective_id=0, has_side_effects=True, vmem_limit_bytes=56 * 1024 * 1024
+            collective_id=0, has_side_effects=True, vmem_limit_bytes=52 * 1024 * 1024
         ),
     )(fill_list, factor_rows, ancestor_inv.reshape(16, 2, 64, 512), diagonal_inv)
 

time: 113 us -> 103 us (0.912)
  Pallas kernels: 109 us -> 97.7 us
    pallas_call x1, Pallas kernels: 109 us -> 97.7 us  [local(): pl.pallas_call(kernel, out_shape=(jax.ShapeDtypeStruct(factor_rows.shape,...]
    unnamed x2 -> x8, local copies, waits for them, and re-layouts: 3.68 us -> 4.29 us
where the time goes in v2:
time: 103 us
  Pallas kernels  97.7 us (95%)
  local copies, waits for them, and re-layouts  4.29 us (4%)
    pallas_call x1, Pallas kernels, local(): pl.pallas_call(kernel, out_shape=(jax.ShapeDtypeStruct(factor_rows.shape,...  97.7 us
    unnamed x8, local copies, waits for them, and re-layouts  4.29 us

profile of v2, /device:TPU:1, one launch (start us, length us, event | category | flops | bytes accessed | tf_op | source)
XLA Modules:
  0.0 102.6 jit_solution(13903849475223982677)
XLA Ops:
  0.6 0.0 copy-start
  0.6 1.1 %copy-done = f32[3,256,256]{2,1,0:T(8,128)S(1)} copy-done((f32[3,256,256]{2,1,0:T(8,128)S(1)}, f32[3,256,256]{2,1,0:T(8,128)}, u32[]{:S(2)}) %copy-start) | copy-done | bytes 786456
  1.8 0.0 copy-start.1
  1.8 0.9 copy-done.1
  2.7 0.0 copy-start.2
  2.7 0.7 copy-done.2
  3.4 97.7 %shard_map.59 = (f32[64,768]{1,0:T(8,128)S(1)}, f32[3,256,256]{2,1,0:T(8,128)S(1)}) custom-call(s32[3,64]{1,0:T(4,128)S(1)} %copy-done.2, f32[64,768]{1,0:T(8,128)S(1)} %copy-done.1, f32[16,2,64,512]{3,2,1,0:T(8,128)} %bitcast.1, f32[3,256,256]{2,1,0:T(8,128)S(1)} %copy-done), custom_call_target="tpu_custom_call" | custom-call | tf_op jit(solution)/shard_map/pallas_call | solution.py:371
  101.0 0.7 copy.8
  101.7 0.9 copy.9
Async XLA Ops:
  0.6 1.1 %copy-start = (f32[3,256,256]{2,1,0:T(8,128)S(1)}, f32[3,256,256]{2,1,0:T(8,128)}, u32[]{:S(2)}) copy-start(f32[3,256,256]{2,1,0:T(8,128)} %d_in.1) | copy-start | bytes 2359300
  1.8 0.9 copy-start.1
  2.7 0.7 copy-start.2

commit v3 on v2

v3 whole, which is shorter than its diff:
```python
import functools

import jax
import jax.numpy as jnp
from jax import lax
from jax.experimental import pallas as pl
from jax.experimental.pallas import tpu as pltpu
from jax.sharding import PartitionSpec as P

W = 256
SIBS = 3
CHUNKS = ((0, 0, 256), (1, 0, 256), (2, 0, 256))
HALF = 128
F32 = jnp.float32
BF16 = jnp.bfloat16


def split(v):
    high = v.astype(BF16)
    return high, (v - high.astype(F32)).astype(BF16)


def three_pass(a_high, a_low, b_high, b_low):
    dot = functools.partial(jnp.dot, preferred_element_type=F32)
    return dot(a_high, b_high) + (dot(a_high, b_low) + dot(a_low, b_high))


def kernel(
    fill, fac, a_in, cb, dg,
    a_own, a_rec, a_high, a_low, m_own, m_rec, m_high, m_low, f_all, t_high, t_low,
    turn, prod, xa, xr, zb, u_out, u_rec, u, rs, zs, g,
    local_sem, turn_s, turn_r, perm_s, perm_r, one_s, one_r, ag_s, ag_r, x_s, x_r, z_s, z_r, c_s, c_r,
    p_s, p_r, e_s, e_r, q_s, q_r, h_s, h_r,
):
    r = lax.axis_index("row")
    c = lax.axis_index("col")
    zl, y = lax.div(r, 4), lax.rem(r, 4)
    x, zh, core = lax.div(c, 8), lax.rem(lax.div(c, 2), 4), lax.rem(c, 2)
    z = zh * 2 + zl
    other = 1 - core
    slab = x * 4 + y

    def wrap(v, n):
        return lax.rem(v + n, n)

    def at(x_, y_, z_, core_):
        return (lax.rem(z_, 2) * 4 + y_, x_ * 8 + lax.div(z_, 2) * 2 + core_)

    def swap(v):
        return v + 1 - 2 * lax.rem(v, 2)

    partner = at(x, y, z, other)
    y_up, y_down = wrap(y + 1, 4), wrap(y - 1, 4)
    y_far = wrap(y + 2, 4)
    up, down = at(x, y_up, z, core), at(x, y_down, z, core)
    right, left = at(wrap(x + 1, 4), y, z, core), at(wrap(x - 1, 4), y, z, core)
    twin = at(x, y, zh * 2 + 1 - zl, core)
    part = lax.div(zh, 2) * 2 + core

    def target(y_from):
        z_to = (2 * lax.rem(y_from, 2) + lax.div(x, 2)) * 2 + 1 - lax.rem(zh, 2)
        return at(2 * zl + lax.div(y_from, 2), y, z_to, lax.rem(x, 2))

    def source(n):
        z_from = ((n // 2) * 2 + 1 - zl) * 2 + lax.div(x, 2)
        return at(2 * lax.rem(zh, 2) + core, y, z_from, n % 2)

    def plane(d):
        return wrap(x + lax.div(d, 4), 4), wrap(y + lax.rem(d, 4), 4)

    barrier = pltpu.get_barrier_semaphore()

    def hello(device):
        pl.semaphore_signal(barrier, inc=1, device_id=device, device_id_type=pl.DeviceIdType.MESH)

    @pl.loop(1, 16)
    def _(d):
        px, py = plane(d)
        hello(at(px, py, z, core))

    @pl.loop(1, 8)
    def _(d):
        hello(at(x, y, wrap(z + d, 8), core))

    hello(partner)
    for n in range(4):
        hello(target(n))
        hello(source(n))

    own_rows = pltpu.make_async_copy(a_in.at[:, core], a_own, local_sem.at[0])
    own_rows.start()
    own_factor = pltpu.make_async_copy(fac, f_all.at[zh], local_sem.at[1])
    own_factor.start()
    def split_rows(src, column):
        @pl.loop(0, 16)
        def _(i):
            rows = pl.ds(pl.multiple_of(i * 64, 64), 64)
            high, low = split(src[i])
            a_high[rows, column : column + 512] = high
            a_low[rows, column : column + 512] = low

    own_rows.wait()
    split_rows(a_own, 0)
    pl.semaphore_wait(barrier, 31)

    sent = []

    def copy(src, dst, ssem, rsem, device):
        return pltpu.make_async_remote_copy(
            src_ref=src, dst_ref=dst, send_sem=ssem, recv_sem=rsem,
            device_id=device, device_id_type=pl.DeviceIdType.MESH,
        )

    def send(src, dst, ssem, rsem, device):
        out = copy(src, dst, ssem, rsem, device)
        out.start()
        sent.append(out)

    def arrived(dst, ssem, rsem):
        copy(dst, dst, ssem, rsem, partner).wait_recv()


    def columns(i):
        k, first, width = CHUNKS[i]
        return k, pl.ds(first, width), first, width

    def quarter(i, n):
        k, _, first, width = columns(i)
        return fac.at[pl.ds(pl.multiple_of(n * 16, 16), 16), pl.ds(k * W + first, width)]

    def forward(i, n, y_from, src):
        k, cut, _, _ = columns(i)
        landing = m_own.at[k, y, 1 - lax.rem(zh, 2), pl.ds(pl.multiple_of(part * 16, 16), 16), cut]
        send(src, landing, perm_s.at[i, n], perm_r.at[i, part], target(y_from))

    for i in range(len(CHUNKS)):
        k, cut, _, _ = columns(i)
        for d in (2, 1, 3):
            y_to = wrap(y + d, 4)
            to = at(x, y_to, z, core)
            send(quarter(i, y_to), turn.at[k, y, :, cut], turn_s.at[i, d - 1], turn_r.at[i, d - 1], to)
        forward(i, 0, y, quarter(i, y))
    send(a_in.at[:, other], a_rec, one_s.at[0], one_r.at[0], partner)

    def split_received(_):
        arrived(a_rec, one_s.at[0], one_r.at[0])
        split_rows(a_rec, 512)

    def ag(i, n, src, dst, device):
        send(src, dst, ag_s.at[i, n], ag_r.at[i, n], device)

    def ag_in(i, n, dst):
        arrived(dst, ag_s.at[i, n], ag_r.at[i, n])

    def one(ref, i, m, half):
        k, cut, _, _ = columns(i)
        return ref.at[k, m, half, :, cut]

    def both(ref, i, m):
        k, cut, _, _ = columns(i)
        return ref.at[k, m, :, :, cut]

    def turned(i):
        k, cut, _, _ = columns(i)
        for d in (1, 3, 2):
            y_from = wrap(y - d, 4)
            landed = turn.at[k, y_from, :, cut]
            arrived(landed, turn_s.at[i, d - 1], turn_r.at[i, d - 1])
            forward(i, d, y_from, landed)

    def gather_a(i):
        k, cut, _, _ = columns(i)
        own = one(m_own, i, y, zl)
        for n in range(4):
            arrived(m_own.at[k, y, zl, pl.ds(n * 16, 16), cut], perm_s.at[i, n], perm_r.at[i, n])
        ag(i, 0, own, own, twin)
        ag(i, 1, own, own, up)
        ag(i, 2, own, own, down)
        ag(i, 3, own, one(m_rec, i, y, zl), partner)

    def gather_b(i):
        own = one(m_own, i, y, 1 - zl)
        ag_in(i, 0, own)
        ag(i, 4, own, own, up)
        ag(i, 5, own, own, down)
        ag(i, 6, own, one(m_rec, i, y, 1 - zl), partner)

    def gather_c(i):
        low = one(m_own, i, y_down, zl)
        ag_in(i, 1, low)
        ag(i, 7, low, low, up)
        high = one(m_own, i, y_up, 1 - zl)
        ag_in(i, 5, high)
        ag(i, 8, high, high, down)

    def gather_d(i):
        ag_in(i, 4, one(m_own, i, y_down, 1 - zl))
        ag(i, 9, both(m_own, i, y_down), both(m_rec, i, y_down), partner)
        ag_in(i, 2, one(m_own, i, y_up, zl))
        ag(i, 10, both(m_own, i, y_up), both(m_rec, i, y_up), partner)
        ag_in(i, 7, one(m_own, i, y_far, zl))
        ag_in(i, 8, one(m_own, i, y_far, 1 - zl))
        ag(i, 11, both(m_own, i, y_far), both(m_rec, i, y_far), partner)

    def split_pieces(i, src, column, start):
        k, _, first, width = columns(i)
        cut = slice(first, first + width)
        for n in range(4):
            mask = fill[k, 2 * column + n // 2].astype(F32)
            for half in range(2):
                piece = (n // 2) * 4 + (1 - half) * 2 + n % 2
                for m in range(4):
                    row = start + piece * 64 + m * 16
                    high, low = split(src[k, m, half, n * 16 : n * 16 + 16, cut] * mask)
                    m_high[k, row : row + 16, cut] = high
                    m_low[k, row : row + 16, cut] = low

    def gather_e(i):
        split_pieces(i, m_own, c, 0)
        ag_in(i, 3, one(m_rec, i, y, zl))
        ag_in(i, 6, one(m_rec, i, y, 1 - zl))
        ag_in(i, 9, both(m_rec, i, y_down))
        ag_in(i, 10, both(m_rec, i, y_up))
        ag_in(i, 11, both(m_rec, i, y_far))
        split_pieces(i, m_rec, swap(c), 512)

    own_tile = r * 8 + lax.div(c, 4)

    def share_factor(_):
        for d in (2, 1, 3):
            to = at(x, y, wrap(zh + d, 4) * 2 + zl, core)
            send(fac, f_all.at[zh], one_s.at[d], one_r.at[d], to)

    def own_masks(_):
        own_factor.wait()
        for d in range(1, 4):
            arrived(f_all.at[wrap(zh - d, 4)], one_s.at[d], one_r.at[d])
        for k in range(SIBS):
            for n in range(4):
                mask = fill[k, r * 8 + x * 2 + n // 2].astype(F32)
                high, low = split((f_all[n, :, k * W : (k + 1) * W] * (mask * mask)).T)
                t_high[k, :, n * 64 : (n + 1) * 64] = high
                t_low[k, :, n * 64 : (n + 1) * 64] = low

    def multiply(i, away):
        k, _, first, width = columns(i)
        cut = slice(first, first + width)
        rows = pl.ds(pl.multiple_of(wrap(x + away, 4) * 256, 256), 256)
        result = three_pass(a_high[rows, :], a_low[rows, :], m_high[k, :, cut], m_low[k, :, cut])
        prod[k, away, :, :, cut] = result.reshape(4, 64, width)

    def x_own(i):
        multiply(i, 0)

    def xs(i, n, away, pair, device):
        k, cut, _, _ = columns(i)
        send(prod.at[k, away, pl.ds(pair, 2), :, cut], xa.at[k, n, :, :, cut], x_s.at[i, n], x_r.at[i, n], device)

    def x_in(i, n):
        k, cut, _, _ = columns(i)
        arrived(xa.at[k, n, :, :, cut], x_s.at[i, n], x_r.at[i, n])

    def x_one(i):
        multiply(i, 2)
        xs(i, 0, 2, 0, right)
        xs(i, 1, 2, 2, left)

    def x_two(i):
        multiply(i, 1)
        xs(i, 2, 1, 2, right)
        multiply(i, 3)
        xs(i, 3, 3, 0, left)

    def x_three(i):
        k, _, first, width = columns(i)
        cut = slice(first, first + width)
        x_in(i, 0)
        prod[k, 1, 0:2, :, cut] = prod[k, 1, 0:2, :, cut] + xa[k, 0, :, :, cut]
        xs(i, 4, 1, 0, right)
        x_in(i, 1)
        prod[k, 3, 2:4, :, cut] = prod[k, 3, 2:4, :, cut] + xa[k, 1, :, :, cut]
        xs(i, 5, 3, 2, left)

    def x_sum(i):
        k, lanes, first, width = columns(i)
        cut = slice(first, first + width)
        x_in(i, 3)
        x_in(i, 4)
        xr[k, 0:2, :, cut] = prod[k, 0, 0:2, :, cut] + xa[k, 4, :, :, cut] + xa[k, 3, :, :, cut]
        x_in(i, 2)
        x_in(i, 5)
        xr[k, 2:4, :, cut] = prod[k, 0, 2:4, :, cut] + xa[k, 2, :, :, cut] + xa[k, 5, :, :, cut]
        for d in (2, 1, 3):
            there = wrap(zh + d, 4)
            to = at(x, y, there * 2 + zl, core)
            send(xr.at[k, there, :, lanes], zb.at[k, d - 1, :, lanes], z_s.at[i, d - 1], z_r.at[i, d - 1], to)

    def z_sum(i):
        k, lanes, first, width = columns(i)
        cut = slice(first, first + width)
        for d in range(3):
            arrived(zb.at[k, d, :, lanes], z_s.at[i, d], z_r.at[i, d])
        mask = fill[k, own_tile].astype(F32)
        block = -(xr[k, zh, :, cut] + zb[k, 0, :, cut] + zb[k, 1, :, cut] + zb[k, 2, :, cut]) * mask
        cb[:, k * W + first : k * W + first + width] = block

    def local_term(i):
        k, lanes, first, width = columns(i)
        cut = slice(first, first + width)
        high, low = split(xr[k, :, :, cut].reshape(W, width))
        whole = three_pass(t_high[k], t_low[k], high, low)
        u_out[k, 0, :, :, cut] = whole[:HALF].reshape(16, 8, width)
        u_out[k, 1, :, :, cut] = whole[HALF:].reshape(16, 8, width)
        send(u_out.at[k, other, :, :, lanes], u_rec.at[k, :, :, lanes], c_s.at[i], c_r.at[i], partner)

    def chip_term(i):
        k, lanes, first, width = columns(i)
        cut = slice(first, first + width)
        arrived(u_rec.at[k, :, :, lanes], c_s.at[i], c_r.at[i])
        u[k, :, :, cut] = u_out[k, core, :, :, cut] + u_rec[k, :, :, cut]

        @pl.loop(1, 16)
        def _(d):
            px, py = plane(d)
            src, dst = u.at[k, px * 4 + py, :, lanes], rs.at[k, d, :, lanes]
            copy(src, dst, p_s.at[i, d], p_r.at[i, d], at(px, py, z, core)).start()

    def plane_sum(i):
        k, lanes, first, width = columns(i)
        cut = slice(first, first + width)
        total = u[k, slab, :, cut]
        for d in range(1, 16):
            arrived(rs.at[k, d, :, lanes], p_s.at[i, d], p_r.at[i, d])
            total = total + rs[k, d, :, cut]
        zs[k, z, :, cut] = total

        @pl.loop(1, 8)
        def _(d):
            mine = zs.at[k, z, :, lanes]
            copy(mine, mine, e_s.at[i, d], e_r.at[i, d], at(x, y, wrap(z + d, 8), core)).start()

    def line_sum(i):
        k, lanes, first, width = columns(i)
        cut = slice(first, first + width)

        @pl.loop(1, 8)
        def _(d):
            arrived(zs.at[k, wrap(z - d, 8), :, lanes], e_s.at[i, d], e_r.at[i, d])

        total = zs[k, 0, :, cut]
        for n in range(1, 8):
            total = total + zs[k, n, :, cut]
        g[k, core, slab, :, cut] = total

        @pl.loop(1, 16)
        def _(d):
            px, py = plane(d)
            mine = g.at[k, core, slab, :, lanes]
            copy(mine, mine, q_s.at[i, d], q_r.at[i, d], at(px, py, z, core)).start()

    def spread(i):
        k, lanes, _, _ = columns(i)

        @pl.loop(1, 16)
        def _(d):
            px, py = wrap(x - lax.div(d, 4), 4), wrap(y - lax.rem(d, 4), 4)
            arrived(g.at[k, core, px * 4 + py, :, lanes], q_s.at[i, d], q_r.at[i, d])

        mine = g.at[k, core, :, :, lanes]
        send(mine, mine, h_s.at[i], h_r.at[i], partner)

    def finish(i):
        k, lanes, first, width = columns(i)
        cut = slice(first, first + width)
        arrived(g.at[k, other, :, :, lanes], h_s.at[i], h_r.at[i])
        for n in range(2):
            dg[k, n * HALF : (n + 1) * HALF, cut] = g[k, n, :, :, cut].reshape(HALF, width)

    order = [
        (turned, 0), (turned, 1), (gather_a, 0), (turned, 2),
        (gather_b, 0), (gather_a, 1), (split_received, 0), (gather_c, 0),
        (gather_b, 1), (gather_a, 2), (gather_d, 0), (gather_c, 1),
        (gather_b, 2), (share_factor, 0), (gather_e, 0), (x_one, 0),
        (x_two, 0), (gather_d, 1), (gather_c, 2), (gather_e, 1),
        (x_one, 1), (x_three, 0), (x_two, 1), (gather_d, 2),
        (gather_e, 2), (x_one, 2), (x_three, 1), (x_two, 2),
        (x_own, 0), (x_own, 1), (x_sum, 0), (x_three, 2),
        (x_own, 2), (own_masks, 0), (local_term, 0), (chip_term, 0),
        (z_sum, 0), (x_sum, 1), (local_term, 1), (chip_term, 1),
        (x_sum, 2), (local_term, 2), (plane_sum, 0), (chip_term, 2),
        (z_sum, 1), (plane_sum, 1), (line_sum, 0), (z_sum, 2),
        (plane_sum, 2), (line_sum, 1), (spread, 0), (line_sum, 2),
        (spread, 1), (spread, 2), (finish, 0), (finish, 1),
        (finish, 2),
    ]
    for step, i in order:
        step(i)

    for out in sent:
        out.wait_send()
    for i in range(len(CHUNKS)):
        k, lanes, _, _ = columns(i)

        @pl.loop(1, 16)
        def _(d):
            copy(u.at[k, 0, :, lanes], rs.at[k, d, :, lanes], p_s.at[i, d], p_r.at[i, d], partner).wait_send()
            mine = g.at[k, core, slab, :, lanes]
            copy(mine, mine, q_s.at[i, d], q_r.at[i, d], partner).wait_send()

        @pl.loop(1, 8)
        def _(d):
            mine = zs.at[k, z, :, lanes]
            copy(mine, mine, e_s.at[i, d], e_r.at[i, d], partner).wait_send()


def local(ancestor_inv, factor_rows, diagonal_inv, fill_list):
    vmem, dma = pltpu.VMEM, pltpu.SemaphoreType.DMA
    hbm = pl.BlockSpec(memory_space=pl.ANY)
    n = len(CHUNKS)
    pairs = [(n, 3), (n, 4), (4,), (n, 12), (n, 6), (n, 3), (n,), (n, 16), (n, 8), (n, 16), (n,)]
    block, update = pl.pallas_call(
        kernel,
        out_shape=(
            jax.ShapeDtypeStruct(factor_rows.shape, F32),
            jax.ShapeDtypeStruct(diagonal_inv.shape, F32),
        ),
        in_specs=[pl.BlockSpec(memory_space=pltpu.SMEM), hbm, hbm],
        out_specs=[pl.BlockSpec(memory_space=pltpu.VMEM)] * 2,
        scratch_shapes=[
            vmem((16, 64, 512), F32),
            vmem((16, 64, 512), F32),
            vmem((1024, 1024), BF16),
            vmem((1024, 1024), BF16),
            vmem((SIBS, 4, 2, 64, W), F32),
            vmem((SIBS, 4, 2, 64, W), F32),
            vmem((SIBS, 1024, W), BF16),
            vmem((SIBS, 1024, W), BF16),
            vmem((4, 64, SIBS * W), F32),
            vmem((SIBS, W, W), BF16),
            vmem((SIBS, W, W), BF16),
            vmem((SIBS, 4, 16, W), F32),
            vmem((SIBS, 4, 4, 64, W), F32),
            vmem((SIBS, 6, 2, 64, W), F32),
            vmem((SIBS, 4, 64, W), F32),
            vmem((SIBS, 3, 64, W), F32),
            vmem((SIBS, 2, 16, 8, W), F32),
            vmem((SIBS, 16, 8, W), F32),
            vmem((SIBS, 16, 8, W), F32),
            vmem((SIBS, 16, 8, W), F32),
            vmem((SIBS, 8, 8, W), F32),
            vmem((SIBS, 2, 16, 8, W), F32),
            dma((2,)),
        ]
        + [dma(shape) for shape in pairs for _ in range(2)],
        compiler_params=pltpu.CompilerParams(
            collective_id=0, has_side_effects=True, vmem_limit_bytes=52 * 1024 * 1024
        ),
    )(fill_list, factor_rows, ancestor_inv.reshape(16, 2, 64, 512))
    return block, diagonal_inv + update


def solution(mesh):
    placed = (P("row", "col"), P(("row", "col"), None), P(), P())
    return jax.shard_map(
        local, mesh=mesh, in_specs=placed, out_specs=(P(("row", "col"), None), P()), check_vma=False
    )
```

time: 103 us -> 97.6 us (0.948)
  Pallas kernels: 97.7 us -> 93.5 us
  local copies, waits for them, and re-layouts: 4.29 us -> 2.28 us
    pallas_call x1, Pallas kernels: 97.7 us -> 93.5 us  [local(): pl.pallas_call(kernel, out_shape=(jax.ShapeDtypeStruct(factor_rows.shape,...]
    unnamed x8 -> x7, local copies, waits for them, and re-layouts: 4.29 us -> 2.28 us
where the time goes in v3:
time: 97.6 us; the launch traced here: 97.4 us
  Pallas kernels  93.5 us (96%)
  local copies, waits for them, and re-layouts  2.28 us (2%)
  other arithmetic  0.98 us (1%)
    pallas_call x1, Pallas kernels, local(): pl.pallas_call(kernel, out_shape=(jax.ShapeDtypeStruct(factor_rows.shape,...  93.5 us
    unnamed x7, local copies, waits for them, and re-layouts  2.28 us

profile of v3, /device:TPU:1, one launch (start us, length us, event | category | flops | bytes accessed | tf_op | source)
XLA Modules:
  0.0 97.4 jit_solution(9910254405973369344)
XLA Ops:
  0.6 0.0 copy-start
  0.6 0.9 copy-done
  1.6 0.0 copy-start.1
  1.6 0.7 copy-done.1
  2.2 0.0 copy-start.2
  2.2 93.5 %shard_map.59 = (f32[64,768]{1,0:T(8,128)S(1)}, f32[3,256,256]{2,1,0:T(8,128)S(1)}) custom-call(s32[3,64]{1,0:T(4,128)S(1)} %copy-done.1, f32[64,768]{1,0:T(8,128)S(1)} %copy-done, f32[16,2,64,512]{3,2,1,0:T(8,128)} %bitcast.1), custom_call_target="tpu_custom_call" | custom-call | tf_op jit(solution)/shard_map/pallas_call | solution.py:421
  95.8 0.0 copy-done.2
  95.8 1.0 %add.3 = f32[3,256,256]{2,1,0:T(8,128)} add(f32[3,256,256]{2,1,0:T(8,128)S(1)} %copy-done.2, f32[3,256,256]{2,1,0:T(8,128)S(1)} %get-tuple-element.5) | non-fusion elementwise | flops 196608 | bytes 2359296 | tf_op jit(solution)/shard_map/add | solution.py:459
  96.8 0.7 copy.7
Async XLA Ops:
  0.6 0.9 copy-start
  1.6 0.7 copy-start.1
  2.2 93.5 %copy-start.2 = (f32[3,256,256]{2,1,0:T(8,128)S(1)}, f32[3,256,256]{2,1,0:T(8,128)}, u32[]{:S(2)}) copy-start(f32[3,256,256]{2,1,0:T(8,128)} %param.6) | copy-start | bytes 2359300

commit v4 on v3

--- a/solution.py
+++ b/solution.py
@@ -385,11 +385,11 @@
         (x_one, 1), (x_three, 0), (x_two, 1), (gather_d, 2),
         (gather_e, 2), (x_one, 2), (x_three, 1), (x_two, 2),
         (x_own, 0), (x_own, 1), (x_sum, 0), (x_three, 2),
-        (x_own, 2), (own_masks, 0), (local_term, 0), (chip_term, 0),
-        (z_sum, 0), (x_sum, 1), (local_term, 1), (chip_term, 1),
-        (x_sum, 2), (local_term, 2), (plane_sum, 0), (chip_term, 2),
-        (z_sum, 1), (plane_sum, 1), (line_sum, 0), (z_sum, 2),
-        (plane_sum, 2), (line_sum, 1), (spread, 0), (line_sum, 2),
+        (x_own, 2), (x_sum, 1), (own_masks, 0), (local_term, 0),
+        (local_term, 1), (chip_term, 0), (chip_term, 1), (x_sum, 2),
+        (local_term, 2), (z_sum, 0), (chip_term, 2), (plane_sum, 0),
+        (plane_sum, 1), (z_sum, 1), (line_sum, 0), (plane_sum, 2),
+        (z_sum, 2), (line_sum, 1), (spread, 0), (line_sum, 2),
         (spread, 1), (spread, 2), (finish, 0), (finish, 1),
         (finish, 2),
     ]

time: 97.6 us -> 97.1 us (level)
  no operation moved by 1% of the time
where the time goes in v4:
time: 97.1 us; the launch traced here: 96.9 us
  Pallas kernels  93 us (96%)
  local copies, waits for them, and re-layouts  2.28 us (2%)
  other arithmetic  0.98 us (1%)
    pallas_call x1, Pallas kernels, local(): pl.pallas_call(kernel, out_shape=(jax.ShapeDtypeStruct(factor_rows.shape,...  93 us
    unnamed x7, local copies, waits for them, and re-layouts  2.28 us

profile of v4, /device:TPU:1, one launch (start us, length us, event | category | flops | bytes accessed | tf_op | source)
XLA Modules:
  0.0 96.9 jit_solution(3558946095269882550)
XLA Ops:
  0.6 0.0 copy-start
  0.6 0.9 copy-done
  1.6 0.0 copy-start.1
  1.6 0.7 copy-done.1
  2.2 0.0 copy-start.2
  2.2 93.0 %shard_map.59 = (f32[64,768]{1,0:T(8,128)S(1)}, f32[3,256,256]{2,1,0:T(8,128)S(1)}) custom-call(s32[3,64]{1,0:T(4,128)S(1)} %copy-done.1, f32[64,768]{1,0:T(8,128)S(1)} %copy-done, f32[16,2,64,512]{3,2,1,0:T(8,128)} %bitcast.1), custom_call_target="tpu_custom_call" | custom-call | tf_op jit(solution)/shard_map/pallas_call | solution.py:421
  95.2 0.0 copy-done.2
  95.2 1.0 %add.3 = f32[3,256,256]{2,1,0:T(8,128)} add(f32[3,256,256]{2,1,0:T(8,128)S(1)} %copy-done.2, f32[3,256,256]{2,1,0:T(8,128)S(1)} %get-tuple-element.5) | non-fusion elementwise | flops 196608 | bytes 2359296 | tf_op jit(solution)/shard_map/add | solution.py:459
  96.2 0.7 copy.7
Async XLA Ops:
  0.6 0.9 copy-start
  1.6 0.7 copy-start.1
  2.2 93.0 %copy-start.2 = (f32[3,256,256]{2,1,0:T(8,128)S(1)}, f32[3,256,256]{2,1,0:T(8,128)}, u32[]{:S(2)}) copy-start(f32[3,256,256]{2,1,0:T(8,128)} %param.6) | copy-start | bytes 2359300
